TPU v7x, 32 devices: a whole 2x2x4 slice. The times are simulated.
32 devices in a mesh: seq: 8 (over y, x, core), tp: 4 (over z).
Axes of the slice: x: 2, y: 2, z: 4, core: 2. Of those that a mesh axis runs over, the one named last changes fastest.
Arguments:
- hidden_in: bfloat16 [8192, 2048], P('seq', 'tp'), may hold values from -6 to 6
- segment_ids: int32 [8192], P('seq'), may hold values from 0 to 7, never falling along the last dimension, each value on 1 to 4096 neighbouring positions
- first_gain: float32 [2048], replicated, may hold values from 0.5 to 1.5
- input_weight: bfloat16 [2048, 2816], P(None, 'tp'), may hold values from -0.125 to 0.125
- gelu_weight: bfloat16 [2048, 2816], P(None, 'tp'), may hold values from -0.125 to 0.125
- conv_weight: float32 [4, 2816], P(None, 'tp'), may hold values from -3 to 3
- conv_bias: float32 [2816], P('tp'), may hold values from -3 to 3
- recur_gate: bfloat16 [16, 176, 176], P('tp'), may hold values from -0.4375 to 0.4375
- input_gate: bfloat16 [16, 176, 176], P('tp'), may hold values from -0.4375 to 0.4375
- recur_bias: float32 [2816], P('tp'), may hold values from -4 to 4
- input_bias: float32 [2816], P('tp'), may hold values from -4 to 4
- decay_param: float32 [2816], P('tp'), may hold values from 5 to 15
- output_weight: bfloat16 [2816, 2048], P('tp'), may hold values from -0.3125 to 0.3125
- second_gain: float32 [2048], replicated, may hold values from 0.5 to 1.5
- gate_weight: bfloat16 [2048, 6144], P('seq', 'tp'), may hold values from -0.125 to 0.125
- up_weight: bfloat16 [2048, 6144], P('seq', 'tp'), may hold values from -0.125 to 0.125
- down_weight: bfloat16 [6144, 2048], P('tp', 'seq'), may hold values from -0.109375 to 0.109375
- grad_out: bfloat16 [8192, 2048], P('seq'), may hold values from -6 to 6
Outputs:
- block_out: bfloat16 [8192, 2048], P('seq', 'tp')
- grad_in: bfloat16 [8192, 2048], P('seq', 'tp')
- grad_first_gain: float32 [2048], replicated
- grad_input_weight: float32 [2048, 2816], P(None, 'tp')
- grad_gelu_weight: float32 [2048, 2816], P(None, 'tp')
- grad_conv_weight: float32 [4, 2816], P(None, 'tp')
- grad_conv_bias: float32 [2816], P('tp')
- grad_recur_gate: float32 [16, 176, 176], P('tp')
- grad_input_gate: float32 [16, 176, 176], P('tp')
- grad_recur_bias: float32 [2816], P('tp')
- grad_input_bias: float32 [2816], P('tp')
- grad_decay: float32 [2816], P('tp')
- grad_output_weight: float32 [2816, 2048], P('tp')
- grad_second_gain: float32 [2048], replicated
- grad_gate_weight: float32 [2048, 6144], P('seq', 'tp')
- grad_up_weight: float32 [2048, 6144], P('seq', 'tp')
- grad_down_weight: float32 [6144, 2048], P('tp', 'seq')
- final_states: float32 [8, 2816], P(None, 'tp')
Inputs may be any that keep to these rules, and one draw needn't show every extreme that they name: `segment_ids`: Non-decreasing along the stream; every segment number occurs; each segment has 1 to 4096 tokens and one has exactly 4096.
All inputs are finite; a program needn't handle non-finite values.
Results may differ from a plain program's by a relative error of at most 0.009.
Values may be sent and summed in bfloat16 or wider, within the bound.
No kernel may reach another device: no remote copies, remote signals or barrier semaphores. Data moves between devices by JAX's collectives and lax.ppermute only.
A program may use at most 448 MiB of HBM per device.

v0:
```python
from functools import partial
import jax
import jax.numpy as jnp
from jax import lax
from jax.sharding import PartitionSpec as P

SEGS = 8
EPSILON = 1e-06
DECAY_SCALE = 8.0


def shifted(x, axis, by):
    peers = lax.axis_size(axis)
    pairs = [(i, i + by) for i in range(peers) if 0 <= i + by < peers]
    return lax.ppermute(x, axis, pairs)


def prefix(part, axis, combine, identity, reverse):
    count = lax.axis_size(axis)
    place = lax.axis_index(axis)
    ahead = count - 1 - place if reverse else place
    gathered = jax.tree.map(lambda a: lax.all_gather(a, axis), part)
    state = jax.tree.map(lambda a, e: jnp.zeros_like(a) + jnp.asarray(e, a.dtype), part, identity)

    def one(hop, state):
        source = count - 1 - hop if reverse else hop
        return combine(
            state, jax.tree.map(lambda a: lax.dynamic_index_in_dim(a, source, 0, False), gathered)
        )

    return lax.fori_loop(0, ahead, one, state)


def rms_norm(value, gain):
    return value * lax.rsqrt(jnp.mean(value * value, axis=1, keepdims=True) + EPSILON) * gain


def compose(earlier, later):
    return (earlier[0] * later[0], later[0] * earlier[1] + later[1])


def gate_math(pre_recur, pre_input, conv_val, bias_recur, bias_input, decay_value, restart):
    rate_gate = jax.nn.sigmoid(pre_recur + bias_recur)
    in_gate = jax.nn.sigmoid(pre_input + bias_input)
    log_decay = -DECAY_SCALE * rate_gate * jax.nn.softplus(-decay_value)
    carried = jnp.where(restart, 0.0, jnp.exp(log_decay))
    scaled = jnp.where(restart, 1.0, jnp.sqrt(-jnp.expm1(2.0 * log_decay)))
    return (carried, scaled * in_gate * conv_val)


def contract_first(left, right):
    return lax.dot_general(
        left, right, (((0,), (0,)), ((), ())), preferred_element_type=jnp.float32
    )


def contract_last(left, right):
    return lax.dot_general(
        left, right, (((1,), (1,)), ((), ())), preferred_element_type=jnp.float32
    )


def exact_dot(left, right):
    return jnp.dot(left, right, precision=lax.Precision.HIGHEST, preferred_element_type=jnp.float32)


def exact_first(left, right):
    return lax.dot_general(
        left,
        right,
        (((0,), (0,)), ((), ())),
        precision=lax.Precision.HIGHEST,
        preferred_element_type=jnp.float32,
    )


def on_device(
    hidden_in,
    segment_ids,
    first_gain,
    input_weight,
    gelu_weight,
    conv_weight,
    conv_bias,
    recur_gate,
    input_gate,
    recur_bias,
    input_bias,
    decay_param,
    output_weight,
    second_gain,
    gate_weight,
    up_weight,
    down_weight,
    grad_out,
):
    tok_dev = hidden_in.shape[0]
    share_width = hidden_in.shape[1]
    channels = input_weight.shape[1]
    conv_taps = conv_weight.shape[0]
    halo_rows = conv_taps - 1
    seq_devices = lax.axis_size("seq")
    seq_place = lax.axis_index("seq")
    tp_place = lax.axis_index("tp")
    share_start = tp_place * share_width
    first_device = seq_place == 0
    final_device = seq_place == seq_devices - 1
    ids_float = segment_ids.astype(jnp.float32)
    row_grid = lax.broadcasted_iota(jnp.int32, (tok_dev, tok_dev), 0)
    col_grid = lax.broadcasted_iota(jnp.int32, (tok_dev, tok_dev), 1)
    edge_rows = lax.broadcasted_iota(jnp.int32, (tok_dev, halo_rows), 0)
    edge_cols = lax.broadcasted_iota(jnp.int32, (tok_dev, halo_rows), 1)
    token_place = lax.broadcasted_iota(jnp.int32, (tok_dev, 1), 0)
    full_in = lax.all_gather(hidden_in, "tp", axis=1, tiled=True).astype(jnp.float32)
    normed1, norm1_back = jax.vjp(rms_norm, full_in, first_gain)
    normed1_low = normed1.astype(jnp.bfloat16)
    branch_x = jnp.dot(normed1_low, input_weight, preferred_element_type=jnp.float32)
    branch_y = jnp.dot(normed1_low, gelu_weight, preferred_element_type=jnp.float32)
    prev_rows, prev_ids = shifted(
        (branch_x[tok_dev - halo_rows :], ids_float[tok_dev - halo_rows :]), "seq", 1
    )
    prev_ids = jnp.where(first_device, -1.0, prev_ids)
    ext_ids = jnp.concatenate([prev_ids, ids_float])
    same_list = [
        (ext_ids[halo_rows - offset : halo_rows - offset + tok_dev] == ids_float).astype(
            jnp.float32
        )[:, None]
        for offset in range(conv_taps)
    ]
    lag_list = [
        (col_grid == row_grid - offset).astype(jnp.float32) * same_list[offset]
        for offset in range(conv_taps)
    ]
    edge_list = [
        (edge_cols == edge_rows - offset + halo_rows).astype(jnp.float32) * same_list[offset]
        for offset in range(conv_taps)
    ]
    window_list = [
        exact_dot(lag_list[offset], branch_x) + exact_dot(edge_list[offset], prev_rows)
        for offset in range(conv_taps)
    ]
    conv_out = conv_bias + sum(
        (conv_weight[offset] * window_list[offset] for offset in range(conv_taps))
    )
    blocks_here = recur_gate.shape[0]
    block_size = recur_gate.shape[1]
    conv_low = conv_out.astype(jnp.bfloat16).reshape(tok_dev, blocks_here, block_size)
    pre_recur = jnp.einsum(
        "tbi,bij->tbj", conv_low, recur_gate, preferred_element_type=jnp.float32
    ).reshape(tok_dev, channels)
    pre_input = jnp.einsum(
        "tbi,bij->tbj", conv_low, input_gate, preferred_element_type=jnp.float32
    ).reshape(tok_dev, channels)
    restart = same_list[1] == 0.0
    (carried, drive), gate_back = jax.vjp(
        partial(gate_math, restart=restart),
        pre_recur,
        pre_input,
        conv_out,
        recur_bias,
        input_bias,
        decay_param,
    )
    cum_decay, local_state = lax.associative_scan(compose, (carried, drive), axis=0)
    ones_row = jnp.ones((channels,), jnp.float32)
    zero_row = jnp.zeros((channels,), jnp.float32)
    incoming = prefix(
        (cum_decay[tok_dev - 1], local_state[tok_dev - 1]),
        "seq",
        compose,
        (ones_row, zero_row),
        False,
    )
    state = local_state + cum_decay * incoming[1]
    gelu_y, gelu_y_back = jax.vjp(jax.nn.gelu, branch_y)
    mixed_low = (gelu_y * state).astype(jnp.bfloat16)
    branch_part = jnp.dot(mixed_low, output_weight, preferred_element_type=jnp.float32)
    resid1 = full_in + lax.psum(branch_part, "tp")
    normed2, norm2_back = jax.vjp(rms_norm, resid1, second_gain)
    normed2_low = normed2.astype(jnp.bfloat16)
    resid_share = lax.dynamic_slice_in_dim(resid1, share_start, share_width, 1)
    hidden_cols = gate_weight.shape[1]
    weight_pieces = (
        lax.all_gather(gate_weight, "seq", axis=0, tiled=True),
        lax.all_gather(up_weight, "seq", axis=0, tiled=True),
    )
    columns = normed2_low
    gate_pre = jnp.dot(columns, weight_pieces[0], preferred_element_type=jnp.float32)
    up_pre = jnp.dot(columns, weight_pieces[1], preferred_element_type=jnp.float32)
    activated, act_back = jax.vjp(jax.nn.gelu, gate_pre)
    hid_low = (activated * up_pre).astype(jnp.bfloat16)
    mlp_part = jnp.dot(
        hid_low,
        lax.all_gather(down_weight, "seq", axis=1, tiled=True),
        preferred_element_type=jnp.float32,
    )
    mlp_share = lax.psum_scatter(mlp_part, "tp", scatter_dimension=1, tiled=True)
    block_out = (resid_share + mlp_share).astype(jnp.bfloat16)
    grad_full = grad_out.astype(jnp.float32)
    columns = grad_out
    d_hid = contract_last(columns, lax.all_gather(down_weight, "seq", axis=1, tiled=True))
    d_gate_low = act_back(d_hid * up_pre)[0].astype(jnp.bfloat16)
    d_up_low = (d_hid * activated).astype(jnp.bfloat16)
    weight_pieces = lax.all_gather((gate_weight, up_weight), "seq", axis=0, tiled=True)
    d_norm2_part = contract_last(d_gate_low, weight_pieces[0]) + contract_last(
        d_up_low, weight_pieces[1]
    )
    d_norm2 = lax.psum(d_norm2_part, "tp")
    d_resid_from2, grad_second = norm2_back(d_norm2)
    d_resid1 = grad_full + d_resid_from2
    d_resid_low = d_resid1.astype(jnp.bfloat16)
    d_resid_share = lax.dynamic_slice_in_dim(d_resid1, share_start, share_width, 1)
    mlp_grads = lax.psum_scatter(
        jnp.concatenate(
            [
                contract_first(normed2_low, d_gate_low),
                contract_first(normed2_low, d_up_low),
                contract_first(grad_out, hid_low),
            ],
            axis=1,
        ),
        "seq",
        scatter_dimension=0,
        tiled=True,
    )
    grad_gate_weight = mlp_grads[:, :hidden_cols]
    grad_up_weight = mlp_grads[:, hidden_cols : 2 * hidden_cols]
    grad_down_weight = mlp_grads[:, 2 * hidden_cols :].T
    d_mixed = contract_last(d_resid_low, output_weight)
    grad_out_weight = contract_first(mixed_low, d_resid_low)
    d_state = d_mixed * gelu_y
    d_branch_y = gelu_y_back(d_mixed * state)[0]
    lead_matrix = (col_grid == row_grid + 1).astype(jnp.float32)
    last_mark = (token_place == tok_dev - 1).astype(jnp.float32)
    first_mark = (token_place == 0).astype(jnp.float32)
    coefficient = exact_dot(lead_matrix, carried) + last_mark
    rev_decay, local_grad = lax.associative_scan(
        compose, (coefficient, d_state), reverse=True, axis=0
    )
    outgoing = (carried[0] * rev_decay[0], carried[0] * local_grad[0])
    from_above = prefix(outgoing, "seq", compose, (ones_row, zero_row), True)
    d_state_all = local_grad + rev_decay * from_above[1]
    trail_matrix = (col_grid == row_grid - 1).astype(jnp.float32)
    prev_state = exact_dot(trail_matrix, state) + first_mark * incoming[1]
    d_pre_recur, d_pre_input, d_conv_direct, grad_rbias, grad_ibias, grad_decay = gate_back(
        (d_state_all * prev_state, d_state_all)
    )
    d_recur_low = d_pre_recur.astype(jnp.bfloat16).reshape(tok_dev, blocks_here, block_size)
    d_input_low = d_pre_input.astype(jnp.bfloat16).reshape(tok_dev, blocks_here, block_size)
    grad_recur_gate = jnp.einsum(
        "tbi,tbj->bij", conv_low, d_recur_low, preferred_element_type=jnp.float32
    )
    grad_input_gate = jnp.einsum(
        "tbi,tbj->bij", conv_low, d_input_low, preferred_element_type=jnp.float32
    )
    d_conv_gates = jnp.einsum(
        "tbj,bij->tbi", d_recur_low, recur_gate, preferred_element_type=jnp.float32
    ) + jnp.einsum("tbj,bij->tbi", d_input_low, input_gate, preferred_element_type=jnp.float32)
    d_conv = d_conv_direct + d_conv_gates.reshape(tok_dev, channels)
    grad_conv_bias = jnp.sum(d_conv, axis=0)
    grad_conv_weight = jnp.stack(
        [jnp.sum(d_conv * window_list[offset], axis=0) for offset in range(conv_taps)], axis=0
    )
    tap_grads = [conv_weight[offset] * d_conv for offset in range(conv_taps)]
    d_local = sum((exact_first(lag_list[offset], tap_grads[offset]) for offset in range(conv_taps)))
    d_edge = sum((exact_first(edge_list[offset], tap_grads[offset]) for offset in range(conv_taps)))
    back_rows, next_first = shifted((d_edge, ids_float[:1]), "seq", -1)
    tail_matrix = (edge_rows == tok_dev - halo_rows + edge_cols).astype(jnp.float32)
    d_branch_x = d_local + exact_dot(tail_matrix, back_rows)
    d_x_low = d_branch_x.astype(jnp.bfloat16)
    d_y_low = d_branch_y.astype(jnp.bfloat16)
    grad_in_weight = contract_first(normed1_low, d_x_low)
    grad_gelu_weight = contract_first(normed1_low, d_y_low)
    d_norm1_part = contract_last(d_x_low, input_weight) + contract_last(d_y_low, gelu_weight)
    d_norm1 = lax.psum(d_norm1_part, "tp")
    d_in_from1, grad_first = norm1_back(d_norm1)
    grad_in = (
        d_resid_share + lax.dynamic_slice_in_dim(d_in_from1, share_start, share_width, 1)
    ).astype(jnp.bfloat16)
    next_first = jnp.where(final_device, -1.0, next_first)
    next_ids = jnp.concatenate([ids_float[1:], next_first])
    segment_ends = (next_ids != ids_float).astype(jnp.float32)[:, None]
    member = (segment_ids[:, None] == jnp.arange(SEGS, dtype=jnp.int32)[None, :]).astype(
        jnp.float32
    )
    final_part = lax.dot_general(
        member,
        state * segment_ends,
        (((0,), (0,)), ((), ())),
        precision=lax.Precision.HIGHEST,
        preferred_element_type=jnp.float32,
    )
    summed = lax.psum(
        (
            grad_in_weight,
            grad_gelu_weight,
            grad_out_weight,
            grad_conv_weight,
            grad_conv_bias,
            grad_recur_gate,
            grad_input_gate,
            grad_rbias,
            grad_ibias,
            grad_decay,
            grad_first,
            grad_second,
            final_part,
        ),
        "seq",
    )
    return (
        block_out,
        grad_in,
        summed[10],
        summed[0],
        summed[1],
        summed[3],
        summed[4],
        summed[5],
        summed[6],
        summed[7],
        summed[8],
        summed[9],
        summed[2],
        summed[11],
        grad_gate_weight,
        grad_up_weight,
        grad_down_weight,
        summed[12],
    )


def solution(mesh):
    return jax.shard_map(
        on_device,
        mesh=mesh,
        in_specs=(
            P("seq", "tp"),
            P("seq"),
            P(),
            P(None, "tp"),
            P(None, "tp"),
            P(None, "tp"),
            P("tp"),
            P("tp", None, None),
            P("tp", None, None),
            P("tp"),
            P("tp"),
            P("tp"),
            P("tp", None),
            P(),
            P("seq", "tp"),
            P("seq", "tp"),
            P("tp", "seq"),
            P("seq", None),
        ),
        out_specs=(
            P("seq", "tp"),
            P("seq", "tp"),
            P(),
            P(None, "tp"),
            P(None, "tp"),
            P(None, "tp"),
            P("tp"),
            P("tp", None, None),
            P("tp", None, None),
            P("tp"),
            P("tp"),
            P("tp"),
            P("tp", None),
            P(),
            P("seq", "tp"),
            P("seq", "tp"),
            P("tp", "seq"),
            P(None, "tp"),
        ),
        check_vma=False,
    )
```

profile of v0, /device:TPU:0, one launch (start us, length us, event | category | flops | bytes accessed | tf_op | source)
XLA Modules:
  0.0 4483.2 jit_solution(468092202798711800)
XLA Ops:
  20.0 73.9 %all-gather.9.cloned.1.call-done = bf16[1024,2048]{1,0:T(8,128)(2,1)} async-done(((bf16[1024,512]{1,0:T(8,128)(2,1)}), bf16[1024,2048]{1,0:T(8,128)(2,1)}) %all-gather.9.cloned.1.call-update) | async-done | bytes 4194320 | tf_op jit(solution)/shard_map/all_gather | solution.py:114
  217.2 51.3 %slice.675 = f32[512,704]{0,1:T(8,128)} slice(f32[1024,704]{0,1:T(8,128)} %copy-done.17), slice={[1:1024:2], [0:704:1]} | slice | bytes 2883584 | tf_op jit(solution)/shard_map/slice | solution.py:164
  268.5 51.2 %slice.674 = f32[512,704]{0,1:T(8,128)} slice(f32[1024,704]{0,1:T(8,128)} %copy-done.17), slice={[0:1023:2], [0:704:1]} | slice | bytes 2883584 | tf_op jit(solution)/shard_map/slice | solution.py:164
  323.6 51.6 %slice.677 = f32[512,704]{0,1:T(8,128)} slice(f32[1024,704]{0,1:T(8,128)} %copy-done.16), slice={[0:1023:2], [0:704:1]} | slice | bytes 2883584 | tf_op jit(solution)/shard_map/slice | solution.py:164
  375.2 51.3 %slice.673 = f32[512,704]{0,1:T(8,128)} slice(f32[1024,704]{0,1:T(8,128)} %copy-done.16), slice={[1:1024:2], [0:704:1]} | slice | bytes 2883584 | tf_op jit(solution)/shard_map/slice | solution.py:164
  884.9 51.3 %slice.672 = f32[511,704]{0,1:T(8,128)} slice(f32[1024,704]{0,1:T(8,128)} %copy-done.16), slice={[2:1024:2], [0:704:1]} | slice | bytes 2877952 | tf_op jit(solution)/shard_map/slice | solution.py:164
  1288.0 57.1 %pad.283 = f32[1024,704]{0,1:T(8,128)} pad(f32[512,704]{0,1:T(8,128)} %add.730, f32[]{:T(128)} %constant.114.clone.1), padding=1_0_1x0_0_0 | pad | bytes 4325380 | tf_op jit(solution)/shard_map/pad | solution.py:164
  1354.5 57.2 %pad.282 = f32[1024,704]{0,1:T(8,128)} pad(f32[512,704]{0,1:T(8,128)} %pad_maximum_fusion.2, f32[]{:T(128)} %constant.114.clone.1), padding=0_1_1x0_0_0 | pad | bytes 4325380 | tf_op jit(solution)/shard_map/pad | solution.py:164
  1422.4 57.1 %pad.263 = f32[1024,704]{0,1:T(8,128)} pad(f32[512,704]{0,1:T(8,128)} %add.719, f32[]{:T(128)} %constant.114.clone.1), padding=1_0_1x0_0_0 | pad | bytes 4325380 | tf_op jit(solution)/shard_map/pad | solution.py:164
  1482.4 57.1 %pad.262 = f32[1024,704]{0,1:T(8,128)} pad(f32[512,704]{0,1:T(8,128)} %pad_maximum_fusion.1, f32[]{:T(128)} %constant.114.clone.1), padding=0_1_1x0_0_0 | pad | bytes 4325380 | tf_op jit(solution)/shard_map/pad | solution.py:164
  1569.9 287.2 %all-reduce.87.cloned.1.call-done = f32[1024,2048]{1,0:T(8,128)} async-done(((f32[1024,2048]{1,0:T(8,128)}), f32[1024,2048]{1,0:T(8,128)}) %all-reduce.87.cloned.1.call-update) | async-done | bytes 8388624 | tf_op jit(solution)/shard_map/psum | solution.py:178
  1940.5 51.5 %slice.777 = f32[512,704]{0,1:T(8,128)} slice(f32[1024,704]{0,1:T(8,128)} %copy-done.46), slice={[1:1024:2], [0:704:1]} | slice | bytes 2883584 | tf_op jit(solution)/shard_map/slice | solution.py:237
  2043.2 51.3 %slice.768 = f32[511,704]{0,1:T(8,128)} slice(f32[1024,704]{0,1:T(8,128)} %copy-done.46), slice={[1:1022:2], [0:704:1]} | slice | bytes 2877952 | tf_op jit(solution)/shard_map/slice | solution.py:237
  2146.3 74.1 %all-reduce.89.cloned.1.call-done = f32[1024,2048]{1,0:T(8,128)} async-done(((f32[1024,2048]{1,0:T(8,128)}), f32[1024,2048]{1,0:T(8,128)}) %all-reduce.89.cloned.1.call-update) | async-done | bytes 8388624 | tf_op jit(solution)/shard_map/psum | solution.py:208
  2247.3 51.3 %slice.774 = f32[512,704]{0,1:T(8,128)} slice(f32[1024,704]{0,1:T(8,128)} %get-tuple-element.297), slice={[0:1023:2], [0:704:1]} | slice | bytes 2883584 | tf_op jit(solution)/shard_map/slice | solution.py:237
  2298.6 51.3 %slice.772 = f32[512,704]{0,1:T(8,128)} slice(f32[1024,704]{0,1:T(8,128)} %get-tuple-element.297), slice={[1:1024:2], [0:704:1]} | slice | bytes 2883584 | tf_op jit(solution)/shard_map/slice | solution.py:237
  2682.4 51.3 %slice.846 = f32[511,704]{0,1:T(8,128)} slice(f32[1024,704]{0,1:T(8,128)} %get-tuple-element.297), slice={[1:1022:2], [0:704:1]} | slice | bytes 2877952 | tf_op jit(solution)/shard_map/slice | solution.py:237
  3282.7 57.1 %pad.302 = f32[1024,704]{0,1:T(8,128)} pad(f32[512,704]{0,1:T(8,128)} %pad_maximum_fusion.3, f32[]{:T(128)} %constant.114.clone.1), padding=0_1_1x0_0_0 | pad | bytes 4325380 | tf_op jit(solution)/shard_map/pad | solution.py:237
  3339.8 57.2 %pad.303 = f32[1024,704]{0,1:T(8,128)} pad(f32[512,704]{0,1:T(8,128)} %add.769, f32[]{:T(128)} %constant.114.clone.1), padding=1_0_1x0_0_0 | pad | bytes 4325380 | tf_op jit(solution)/shard_map/pad | solution.py:237
  3430.7 57.1 %pad.322 = f32[1024,704]{0,1:T(8,128)} pad(f32[512,704]{0,1:T(8,128)} %pad_maximum_fusion.4, f32[]{:T(128)} %constant.114.clone.1), padding=0_1_1x0_0_0 | pad | bytes 4325380 | tf_op jit(solution)/shard_map/pad | solution.py:237
  3487.8 57.3 %pad.323 = f32[1024,704]{0,1:T(8,128)} pad(f32[512,704]{0,1:T(8,128)} %add.780, f32[]{:T(128)} %constant.114.clone.1), padding=1_0_1x0_0_0 | pad | bytes 4325380 | tf_op jit(solution)/shard_map/pad | solution.py:237
  3789.2 197.0 %all-reduce.91.cloned.1.call-done = f32[1024,2048]{1,0:T(8,128)} async-done(((f32[1024,2048]{1,0:T(8,128)}), f32[1024,2048]{1,0:T(8,128)}) %all-reduce.91.cloned.1.call-update) | async-done | bytes 8388624 | tf_op jit(solution)/shard_map/psum | solution.py:275
  4025.6 188.5 %reduce-scatter.5.cloned.1.call-done = f32[256,4608]{0,1:T(8,128)} async-done(((f32[2048,4608]{0,1:T(8,128)}), f32[256,4608]{0,1:T(8,128)}) %reduce-scatter.5.cloned.1.call-update) | async-done | bytes 4718608 | tf_op jit(solution)/shard_map/reduce_scatter | solution.py:213
  4224.8 236.9 %all-reduce.93.cloned.1.call-done = (f32[2048,704]{0,1:T(8,128)}, f32[2048,704]{0,1:T(8,128)}, f32[4,176,176]{2,1,0:T(8,128)}, f32[4,176,176]{2,1,0:T(8,128)}, f32[704,2048]{1,0:T(8,128)}) async-done(((f32[2048,704]{0,1:T(8,128)}, f32[2048,704]{0,1:T(8,128)}, f32[4,176,176]{2,1,0:T(8,128)}, f32[4,176,176]{2,1,0:T(8,128)}, f32[704,2048]{1,0:T(8,128)}), (f32[2048,704]{0,1:T(8,128)}, f32[2048,704]{0,1:T(8,128)}, ...) | async-done | bytes 18292752 | tf_op jit(solution)/shard_map/psum | solution.py:293
  (811 shorter events, 2436.5 us)
Async XLA Ops:
  8.0 1542.1 %copy-start = (bf16[2048,704]{0,1:T(8,128)(2,1)S(1)}, bf16[2048,704]{0,1:T(8,128)(2,1)}, u32[]{:S(2)}) copy-start(bf16[2048,704]{0,1:T(8,128)(2,1)} %param.26) | copy-start | bytes 8650756
  8.0 85.9 %all-gather.9.cloned.1.call-start = ((), (), s32[]{:S(2)}) async-start(), calls=%async_computation.2 | async-start | bytes 5242880 | tf_op jit(solution)/shard_map/all_gather | solution.py:114
  8.8 1848.3 %all-reduce.87.cloned.1.call-start = ((), (), s32[]{:S(2)}) async-start(), calls=%async_computation.3 | async-start | bytes 16777216 | tf_op jit(solution)/shard_map/psum | solution.py:178
  9.7 10.2 collective-permute-start
  12.5 5.4 collective-permute-start.3
  14.9 137.5 %copy-start.104 = (f32[704]{0:T(1024)}, f32[704]{0:T(1024)S(1)}, u32[]{:S(2)}) copy-start(f32[704]{0:T(1024)S(1)} %get-tuple-element.233) | copy-start | bytes 8452
  14.9 137.5 %copy-start.106 = (f32[704]{0:T(1024)}, f32[704]{0:T(1024)S(1)}, u32[]{:S(2)}) copy-start(f32[704]{0:T(1024)S(1)} %get-tuple-element.234) | copy-start | bytes 8452
  16.2 303.5 %copy-start.101 = (f32[704]{0:T(1024)}, f32[704]{0:T(1024)S(1)}, u32[]{:S(2)}) copy-start(f32[704]{0:T(1024)S(1)} %get-tuple-element.390) | copy-start | bytes 8452
  20.0 299.7 %copy-start.132 = (pred[1024]{0:T(1024)(128)(4,1)}, pred[1024]{0:T(1024)(128)(4,1)S(1)}, u32[]{:S(2)}) copy-start(pred[1024]{0:T(1024)(128)(4,1)S(1)} %get-tuple-element.284) | copy-start | bytes 3076
  97.8 1452.3 %copy-start.129 = (f32[1024]{0:T(1024)}, f32[1024]{0:T(1024)S(1)}, u32[]{:S(2)}) copy-start(f32[1024]{0:T(1024)S(1)} %fusion.172) | copy-start | bytes 12292
  103.0 41.3 collective-permute-start.1
  1568.1 300.9 %all-gather.13.cloned.1.call-start = ((), (), s32[]{:S(2)}) async-start(), calls=%async_computation.5 | async-start | bytes 7077888 | tf_op jit(solution)/shard_map/all_gather | solution.py:185
  1568.7 312.3 %all-gather.11.cloned.1.call-start = ((), (), s32[]{:S(2)}) async-start(), calls=%async_computation.4 | async-start | bytes 7077888 | tf_op jit(solution)/shard_map/all_gather | solution.py:184
  1569.3 323.5 %all-gather.15.cloned.1.call-start = ((), (), s32[]{:S(2)}) async-start(), calls=%async_computation.6 | async-start | bytes 7077888 | tf_op jit(solution)/shard_map/all_gather | solution.py:194
  1569.8 296.4 %copy-start.103 = (f32[2048]{0:T(1024)S(1)}, f32[2048]{0:T(1024)}, u32[]{:S(2)}) copy-start(f32[2048]{0:T(1024)} %param.35) | copy-start | bytes 24580
  1569.8 650.6 %all-reduce.89.cloned.1.call-start = ((), (), s32[]{:S(2)}) async-start(), calls=%async_computation.8 | async-start | bytes 16777216 | tf_op jit(solution)/shard_map/psum | solution.py:208
  1930.5 1855.1 %reduce-scatter.3.cloned.1.call-start = ((), (), s32[]{:S(2)}) async-start(), calls=%async_computation.7 | async-start | bytes 10485760 | tf_op jit(solution)/shard_map/reduce_scatter | solution.py:197
  2146.3 1839.9 %all-reduce.91.cloned.1.call-start = ((), (), s32[]{:S(2)}) async-start(), calls=%async_computation.9 | async-start | bytes 16777216 | tf_op jit(solution)/shard_map/psum | solution.py:275
  3642.6 42.3 collective-permute-start.2
  3696.2 517.9 %reduce-scatter.5.cloned.1.call-start = ((), (), s32[]{:S(2)}) async-start(), calls=%async_computation.10 | async-start | bytes 42467328 | tf_op jit(solution)/shard_map/reduce_scatter | solution.py:213
  3752.8 708.9 %all-reduce.93.cloned.1.call-start = ((), (), s32[]{:S(2)}) async-start(), calls=%async_computation.11 | async-start | bytes 37486592 | tf_op jit(solution)/shard_map/psum | solution.py:293
  3789.2 205.3 %copy-start.131 = (f32[2048]{0:T(1024)S(1)}, f32[2048]{0:T(1024)}, u32[]{:S(2)}) copy-start(f32[2048]{0:T(1024)} %get-tuple-element.220) | copy-start | bytes 24580
  3789.2 205.3 %copy-start.134 = (f32[704]{0:T(1024)S(1)}, f32[704]{0:T(1024)}, u32[]{:S(2)}) copy-start(f32[704]{0:T(1024)} %get-tuple-element.270) | copy-start | bytes 8452
  3789.2 230.8 %copy-start.127 = (f32[1024]{0:T(1024)S(1)}, f32[1024]{0:T(1024)}, u32[]{:S(2)}) copy-start(f32[1024]{0:T(1024)} %copy-done.126) | copy-start | bytes 12292
  (154 other events, 2792.6 us)
Sparse Core Ops, SparseCore 0:
  10.5 83.4 all-gather.8
  1568.2 288.8 all-reduce.86
  1930.6 289.8 all-reduce.88
  2222.7 143.4 reduce-scatter.2
  3696.3 289.8 all-reduce.90
  3989.7 224.3 reduce-scatter.4
  4220.6 241.0 all-reduce.92
Sparse Core Ops, SparseCore 1:
  1570.4 43.4 all-gather.12
  1615.6 45.3 all-gather.10
  1662.8 46.5 all-gather.14
where the time goes:
time: 4510 us; the launch traced here: 4480 us
  local copies, waits for them, and re-layouts  2710 us (60%)
  waiting for transfers between devices  1060 us (24%)
  other arithmetic  323 us (7%)
  matrix products  302 us (7%)
  blocking collectives  61.7 us (1%)
    slice x63, local copies, waits for them, and re-layouts, on_device(): lax.associative_scan(compose, (coefficient, d_state), reverse=True, axis=0)  809 us
    slice x59, local copies, waits for them, and re-layouts, on_device(): lax.associative_scan(compose, (carried, drive), axis=0)  741 us
    pad x36, local copies, waits for them, and re-layouts, on_device(): lax.associative_scan(compose, (coefficient, d_state), reverse=True, axis=0)  508 us
    pad x36, local copies, waits for them, and re-layouts, on_device(): lax.associative_scan(compose, (carried, drive), axis=0)  500 us
    psum x1, waiting for transfers between devices, on_device(): resid1 = full_in + lax.psum(branch_part, 'tp')  287 us
    psum x1, waiting for transfers between devices, on_device(): lax.psum((grad_in_weight, grad_gelu_weight, grad_out_weight, grad_conv_we...  237 us
    psum x1, waiting for transfers between devices, on_device(): d_norm1 = lax.psum(d_norm1_part, 'tp')  197 us
    reduce_scatter x1, waiting for transfers between devices, on_device(): lax.psum_scatter(jnp.concatenate([contract_first(normed2_low, d_gate_low)...  189 us
  transfers between devices with their start and end apart: 14, of which 7 were waited for; matrix products, arithmetic and copies ran while one was open for 41% of the time, Pallas kernels for 0%

commit v1 on v0

--- a/solution.py
+++ b/solution.py
@@ -175,7 +175,7 @@
     gelu_y, gelu_y_back = jax.vjp(jax.nn.gelu, branch_y)
     mixed_low = (gelu_y * state).astype(jnp.bfloat16)
     branch_part = jnp.dot(mixed_low, output_weight, preferred_element_type=jnp.float32)
-    resid1 = full_in + lax.psum(branch_part, "tp")
+    resid1 = full_in + jnp.sum(lax.all_gather(branch_part, "tp"), axis=0)
     normed2, norm2_back = jax.vjp(rms_norm, resid1, second_gain)
     normed2_low = normed2.astype(jnp.bfloat16)
     resid_share = lax.dynamic_slice_in_dim(resid1, share_start, share_width, 1)

time: 4510 us -> 4890 us (1.084)
  waiting for transfers between devices: 1060 us -> 1420 us
    all_gather x0 -> x1, waiting for transfers between devices: none -> 558 us  [on_device(): resid1 = full_in + jnp.sum(lax.all_gather(branch_part, 'tp'), axis=0)]
    psum x1 -> x0, waiting for transfers between devices: 287 us -> none  [on_device(): resid1 = full_in + lax.psum(branch_part, 'tp')]
  transfers between devices with their start and end apart: 14 -> 14, of which waited for: 7 -> 10; matrix products, arithmetic and copies ran while one was open for 41% -> 39% of each run, Pallas kernels for 0% -> 0%
where the time goes in v1:
time: 4890 us; the launch traced here: 4870 us
  local copies, waits for them, and re-layouts  2710 us (55%)
  waiting for transfers between devices  1420 us (29%)
  other arithmetic  343 us (7%)
  matrix products  305 us (6%)
  blocking collectives  61.7 us (1%)
    slice x63, local copies, waits for them, and re-layouts, on_device(): lax.associative_scan(compose, (coefficient, d_state), reverse=True, axis=0)  809 us
    slice x59, local copies, waits for them, and re-layouts, on_device(): lax.associative_scan(compose, (carried, drive), axis=0)  741 us
    all_gather x1, waiting for transfers between devices, on_device(): resid1 = full_in + jnp.sum(lax.all_gather(branch_part, 'tp'), axis=0)  558 us
    pad x36, local copies, waits for them, and re-layouts, on_device(): lax.associative_scan(compose, (coefficient, d_state), reverse=True, axis=0)  508 us
    pad x36, local copies, waits for them, and re-layouts, on_device(): lax.associative_scan(compose, (carried, drive), axis=0)  506 us
    psum x1, waiting for transfers between devices, on_device(): lax.psum((grad_in_weight, grad_gelu_weight, grad_out_weight, grad_conv_we...  237 us
    psum x1, waiting for transfers between devices, on_device(): d_norm1 = lax.psum(d_norm1_part, 'tp')  197 us
    reduce_scatter x1, waiting for transfers between devices, on_device(): lax.psum_scatter(jnp.concatenate([contract_first(normed2_low, d_gate_low)...  189 us
  transfers between devices with their start and end apart: 14, of which 10 were waited for; matrix products, arithmetic and copies ran while one was open for 39% of the time, Pallas kernels for 0%

profile of v1, /device:TPU:0, one launch (start us, length us, event | category | flops | bytes accessed | tf_op | source)
XLA Modules:
  0.0 4865.3 jit_solution(5706910985519011430)
XLA Ops:
  19.1 74.0 %all-gather.11.cloned.1.call-done = bf16[1024,2048]{1,0:T(8,128)(2,1)} async-done(((bf16[1024,512]{1,0:T(8,128)(2,1)}), bf16[1024,2048]{1,0:T(8,128)(2,1)}) %all-gather.11.cloned.1.call-update) | async-done | bytes 4194320 | tf_op jit(solution)/shard_map/all_gather | solution.py:114
  163.2 51.3 %slice.675 = f32[512,704]{0,1:T(8,128)} slice(f32[1024,704]{0,1:T(8,128)} %get-tuple-element.281), slice={[1:1024:2], [0:704:1]} | slice | bytes 2883584 | tf_op jit(solution)/shard_map/slice | solution.py:164
  214.5 51.2 %slice.674 = f32[512,704]{0,1:T(8,128)} slice(f32[1024,704]{0,1:T(8,128)} %get-tuple-element.281), slice={[0:1023:2], [0:704:1]} | slice | bytes 2883584 | tf_op jit(solution)/shard_map/slice | solution.py:164
  269.6 51.3 %slice.673 = f32[512,704]{0,1:T(8,128)} slice(f32[1024,704]{0,1:T(8,128)} %exponential_select_fusion), slice={[1:1024:2], [0:704:1]} | slice | bytes 2883584 | tf_op jit(solution)/shard_map/slice | solution.py:164
  320.9 51.6 %slice.677 = f32[512,704]{0,1:T(8,128)} slice(f32[1024,704]{0,1:T(8,128)} %exponential_select_fusion), slice={[0:1023:2], [0:704:1]} | slice | bytes 2883584 | tf_op jit(solution)/shard_map/slice | solution.py:164
  1231.2 57.1 %pad.283 = f32[1024,704]{0,1:T(8,128)} pad(f32[512,704]{0,1:T(8,128)} %add.728, f32[]{:T(128)} %constant.114.clone.1), padding=1_0_1x0_0_0 | pad | bytes 4325380 | tf_op jit(solution)/shard_map/pad | solution.py:164
  1357.3 57.2 %pad.282 = f32[1024,704]{0,1:T(8,128)} pad(f32[512,704]{0,1:T(8,128)} %pad_maximum_fusion.2, f32[]{:T(128)} %constant.114.clone.1), padding=0_1_1x0_0_0 | pad | bytes 4325380 | tf_op jit(solution)/shard_map/pad | solution.py:164
  1425.2 57.1 %pad.263 = f32[1024,704]{0,1:T(8,128)} pad(f32[512,704]{0,1:T(8,128)} %add.717, f32[]{:T(128)} %constant.114.clone.1), padding=1_0_1x0_0_0 | pad | bytes 4325380 | tf_op jit(solution)/shard_map/pad | solution.py:164
  1485.2 57.1 %pad.262 = f32[1024,704]{0,1:T(8,128)} pad(f32[512,704]{0,1:T(8,128)} %pad_maximum_fusion.1, f32[]{:T(128)} %constant.114.clone.1), padding=0_1_1x0_0_0 | pad | bytes 4325380 | tf_op jit(solution)/shard_map/pad | solution.py:164
  1572.9 557.7 %all-gather.19.cloned.1.call-done = f32[4096,2048]{1,0:T(8,128)} async-done(((f32[1024,2048]{1,0:T(8,128)}), f32[4096,2048]{1,0:T(8,128)}) %all-gather.19.cloned.1.call-update) | async-done | bytes 33554448 | tf_op jit(solution)/shard_map/all_gather | solution.py:178
  2320.4 51.4 %slice.770 = f32[512,704]{0,1:T(8,128)} slice(f32[1024,704]{0,1:T(8,128)} %fusion.89), slice={[0:1023:2], [0:704:1]} | slice | bytes 2883584 | tf_op jit(solution)/shard_map/slice | solution.py:237
  2371.8 51.3 %slice.777 = f32[512,704]{0,1:T(8,128)} slice(f32[1024,704]{0,1:T(8,128)} %fusion.89), slice={[1:1024:2], [0:704:1]} | slice | bytes 2883584 | tf_op jit(solution)/shard_map/slice | solution.py:237
  2423.2 51.3 %slice.768 = f32[511,704]{0,1:T(8,128)} slice(f32[1024,704]{0,1:T(8,128)} %fusion.89), slice={[1:1022:2], [0:704:1]} | slice | bytes 2877952 | tf_op jit(solution)/shard_map/slice | solution.py:237
  2528.3 74.1 %all-reduce.86.cloned.1.call-done = f32[1024,2048]{1,0:T(8,128)} async-done(((f32[1024,2048]{1,0:T(8,128)}), f32[1024,2048]{1,0:T(8,128)}) %all-reduce.86.cloned.1.call-update) | async-done | bytes 8388624 | tf_op jit(solution)/shard_map/psum | solution.py:208
  2629.2 51.3 %slice.774 = f32[512,704]{0,1:T(8,128)} slice(f32[1024,704]{0,1:T(8,128)} %get-tuple-element.297), slice={[0:1023:2], [0:704:1]} | slice | bytes 2883584 | tf_op jit(solution)/shard_map/slice | solution.py:237
  2680.5 51.3 %slice.772 = f32[512,704]{0,1:T(8,128)} slice(f32[1024,704]{0,1:T(8,128)} %get-tuple-element.297), slice={[1:1024:2], [0:704:1]} | slice | bytes 2883584 | tf_op jit(solution)/shard_map/slice | solution.py:237
  3222.1 51.5 %slice.846 = f32[511,704]{0,1:T(8,128)} slice(f32[1024,704]{0,1:T(8,128)} %get-tuple-element.297), slice={[1:1022:2], [0:704:1]} | slice | bytes 2877952 | tf_op jit(solution)/shard_map/slice | solution.py:237
  3664.9 57.3 %pad.302 = f32[1024,704]{0,1:T(8,128)} pad(f32[512,704]{0,1:T(8,128)} %pad_maximum_fusion.3, f32[]{:T(128)} %constant.114.clone.1), padding=0_1_1x0_0_0 | pad | bytes 4325380 | tf_op jit(solution)/shard_map/pad | solution.py:237
  3722.2 57.3 %pad.303 = f32[1024,704]{0,1:T(8,128)} pad(f32[512,704]{0,1:T(8,128)} %add.767, f32[]{:T(128)} %constant.114.clone.1), padding=1_0_1x0_0_0 | pad | bytes 4325380 | tf_op jit(solution)/shard_map/pad | solution.py:237
  3813.5 57.5 %pad.322 = f32[1024,704]{0,1:T(8,128)} pad(f32[512,704]{0,1:T(8,128)} %pad_maximum_fusion.4, f32[]{:T(128)} %constant.114.clone.1), padding=0_1_1x0_0_0 | pad | bytes 4325380 | tf_op jit(solution)/shard_map/pad | solution.py:237
  3870.9 57.1 %pad.323 = f32[1024,704]{0,1:T(8,128)} pad(f32[512,704]{0,1:T(8,128)} %add.778, f32[]{:T(128)} %constant.114.clone.1), padding=1_0_1x0_0_0 | pad | bytes 4325380 | tf_op jit(solution)/shard_map/pad | solution.py:237
  4171.8 197.3 %all-reduce.88.cloned.1.call-done = f32[1024,2048]{1,0:T(8,128)} async-done(((f32[1024,2048]{1,0:T(8,128)}), f32[1024,2048]{1,0:T(8,128)}) %all-reduce.88.cloned.1.call-update) | async-done | bytes 8388624 | tf_op jit(solution)/shard_map/psum | solution.py:275
  4408.2 188.9 %reduce-scatter.5.cloned.1.call-done = f32[256,4608]{0,1:T(8,128)} async-done(((f32[2048,4608]{0,1:T(8,128)}), f32[256,4608]{0,1:T(8,128)}) %reduce-scatter.5.cloned.1.call-update) | async-done | bytes 4718608 | tf_op jit(solution)/shard_map/reduce_scatter | solution.py:213
  4607.8 236.8 %all-reduce.90.cloned.1.call-done = (f32[2048,704]{0,1:T(8,128)}, f32[2048,704]{0,1:T(8,128)}, f32[4,176,176]{2,1,0:T(8,128)}, f32[4,176,176]{2,1,0:T(8,128)}, f32[704,2048]{1,0:T(8,128)}) async-done(((f32[2048,704]{0,1:T(8,128)}, f32[2048,704]{0,1:T(8,128)}, f32[4,176,176]{2,1,0:T(8,128)}, f32[4,176,176]{2,1,0:T(8,128)}, f32[704,2048]{1,0:T(8,128)}), (f32[2048,704]{0,1:T(8,128)}, f32[2048,704]{0,1:T(8,128)}, ...) | async-done | bytes 18292752 | tf_op jit(solution)/shard_map/psum | solution.py:293
  (774 shorter events, 2548.7 us)
Async XLA Ops:
  7.2 1545.7 %copy-start = (bf16[2048,704]{0,1:T(8,128)(2,1)S(1)}, bf16[2048,704]{0,1:T(8,128)(2,1)}, u32[]{:S(2)}) copy-start(bf16[2048,704]{0,1:T(8,128)(2,1)} %param.26) | copy-start | bytes 8650756
  7.2 85.9 %all-gather.11.cloned.1.call-start = ((), (), s32[]{:S(2)}) async-start(), calls=%async_computation.2 | async-start | bytes 5242880 | tf_op jit(solution)/shard_map/all_gather | solution.py:114
  8.0 2122.7 %all-gather.19.cloned.1.call-start = ((), (), s32[]{:S(2)}) async-start(), calls=%async_computation.10 | async-start | bytes 41943040 | tf_op jit(solution)/shard_map/all_gather | solution.py:178
  8.8 10.2 collective-permute-start
  11.7 5.4 collective-permute-start.3
  14.1 137.6 %copy-start.85 = (f32[704]{0:T(1024)}, f32[704]{0:T(1024)S(1)}, u32[]{:S(2)}) copy-start(f32[704]{0:T(1024)S(1)} %get-tuple-element.233) | copy-start | bytes 8452
  14.1 137.6 %copy-start.87 = (f32[704]{0:T(1024)}, f32[704]{0:T(1024)S(1)}, u32[]{:S(2)}) copy-start(f32[704]{0:T(1024)S(1)} %get-tuple-element.234) | copy-start | bytes 8452
  14.1 137.6 %copy-start.89 = (f32[704]{0:T(1024)}, f32[704]{0:T(1024)S(1)}, u32[]{:S(2)}) copy-start(f32[704]{0:T(1024)S(1)} %get-tuple-element.236) | copy-start | bytes 8452
  15.4 250.3 %copy-start.82 = (f32[704]{0:T(1024)}, f32[704]{0:T(1024)S(1)}, u32[]{:S(2)}) copy-start(f32[704]{0:T(1024)S(1)} %get-tuple-element.390) | copy-start | bytes 8452
  19.1 246.6 %copy-start.113 = (pred[1024]{0:T(1024)(128)(4,1)}, pred[1024]{0:T(1024)(128)(4,1)S(1)}, u32[]{:S(2)}) copy-start(pred[1024]{0:T(1024)(128)(4,1)S(1)} %get-tuple-element.284) | copy-start | bytes 3076
  97.0 1455.9 %copy-start.110 = (f32[1024]{0:T(1024)}, f32[1024]{0:T(1024)S(1)}, u32[]{:S(2)}) copy-start(f32[1024]{0:T(1024)S(1)} %fusion.172) | copy-start | bytes 12292
  102.2 41.3 collective-permute-start.1
  1571.0 605.3 %all-gather.13.cloned.1.call-start = ((), (), s32[]{:S(2)}) async-start(), calls=%async_computation.3 | async-start | bytes 7077888 | tf_op jit(solution)/shard_map/all_gather | solution.py:184
  1571.7 651.8 %all-gather.15.cloned.1.call-start = ((), (), s32[]{:S(2)}) async-start(), calls=%async_computation.4 | async-start | bytes 7077888 | tf_op jit(solution)/shard_map/all_gather | solution.py:185
  1572.3 699.7 %all-gather.17.cloned.1.call-start = ((), (), s32[]{:S(2)}) async-start(), calls=%async_computation.5 | async-start | bytes 7077888 | tf_op jit(solution)/shard_map/all_gather | solution.py:194
  1572.9 1029.5 %all-reduce.86.cloned.1.call-start = ((), (), s32[]{:S(2)}) async-start(), calls=%async_computation.7 | async-start | bytes 16777216 | tf_op jit(solution)/shard_map/psum | solution.py:208
  2311.4 1856.8 %reduce-scatter.3.cloned.1.call-start = ((), (), s32[]{:S(2)}) async-start(), calls=%async_computation.6 | async-start | bytes 10485760 | tf_op jit(solution)/shard_map/reduce_scatter | solution.py:197
  2528.3 1840.9 %all-reduce.88.cloned.1.call-start = ((), (), s32[]{:S(2)}) async-start(), calls=%async_computation.8 | async-start | bytes 16777216 | tf_op jit(solution)/shard_map/psum | solution.py:275
  4025.6 42.3 collective-permute-start.2
  4079.2 518.0 %reduce-scatter.5.cloned.1.call-start = ((), (), s32[]{:S(2)}) async-start(), calls=%async_computation.9 | async-start | bytes 42467328 | tf_op jit(solution)/shard_map/reduce_scatter | solution.py:213
  4135.6 709.0 %all-reduce.90.cloned.1.call-start = ((), (), s32[]{:S(2)}) async-start(), calls=%async_computation.11 | async-start | bytes 37486592 | tf_op jit(solution)/shard_map/psum | solution.py:293
  4171.8 205.4 %copy-start.112 = (f32[2048]{0:T(1024)S(1)}, f32[2048]{0:T(1024)}, u32[]{:S(2)}) copy-start(f32[2048]{0:T(1024)} %get-tuple-element.220) | copy-start | bytes 24580
  4171.8 205.4 %copy-start.115 = (f32[704]{0:T(1024)S(1)}, f32[704]{0:T(1024)}, u32[]{:S(2)}) copy-start(f32[704]{0:T(1024)} %get-tuple-element.270) | copy-start | bytes 8452
  4171.8 230.9 %copy-start.108 = (f32[1024]{0:T(1024)S(1)}, f32[1024]{0:T(1024)}, u32[]{:S(2)}) copy-start(f32[1024]{0:T(1024)} %copy-done.107) | copy-start | bytes 12292
  (135 other events, 2614.9 us)
Sparse Core Ops, SparseCore 0:
  9.6 83.4 all-gather.10
  1571.1 559.4 all-gather.18
  2132.5 43.6 all-gather.12
  2178.0 45.5 all-gather.14
  2225.3 46.6 all-gather.16
  2311.5 290.8 all-reduce.85
  2604.8 143.4 reduce-scatter.2
  4079.3 289.7 all-reduce.87
  4372.7 224.3 reduce-scatter.4
  4603.5 241.0 all-reduce.89
